TPU v7x, 256 devices: a whole 4x4x8 slice. The times are simulated.
256 devices in a mesh: tok: 32 (over z, y), voc: 8 (over x, core).
Axes of the slice: x: 4, y: 4, z: 8, core: 2. Of those that a mesh axis runs over, the one named last changes fastest.
Arguments:
- hidden: bfloat16 [8192, 1536], P('tok'), may hold values from -1000 to 1000
- norm_gain: float32 [1536], replicated, may hold values from 0.1 to 1.9
- head_weight: bfloat16 [1536, 49152], P(None, ('tok', 'voc')), may hold values from -8 to 8
- targets: int32 [8192], P('tok'), may hold values from 0 to 49151
- lengths: int32 [32], replicated, may hold values from 1 to 256, 5120 in all
- prior_device: int32 [32], replicated, may hold values from 0 to 31, each once
- prior_row: int32 [32], replicated, may hold values from 0 to 255
Outputs:
- logprob: float32 [8192], P('tok')
- entropy: float32 [8192], P('tok')
Inputs may be any that keep to these rules, and one draw needn't show every extreme that they name: One turn's block is full, lengths[t] = 256. `prior_device`: every block index appears once.
All inputs are finite; a program needn't handle non-finite values.
Results may differ from a plain program's by a relative error of at most 0.0036.
Values may be sent and summed in bfloat16 or wider, within the bound.
A program may use at most 192 MiB of HBM per device.

v0:
```python
import jax
import jax.numpy as jnp
from jax import lax
from jax.sharding import PartitionSpec as P

epsilon = 1e-05


def select_entry(table, wanted):
    positions = jnp.arange(table.shape[0], dtype=jnp.int32)
    return jnp.sum(jnp.where(positions == wanted, table, 0))


def combine(first, second):
    largest = jnp.maximum(first[0], second[0])
    later = jnp.exp(second[0] - largest)
    return (largest, second[1] * later, second[2] * later, second[3])


def block_size(total_rows):
    for candidate in (512, 384, 256, 128):
        if total_rows % candidate == 0:
            return candidate
    return total_rows


def block_stats(states, columns, target_col):
    total_rows = states.shape[0]
    block_rows = block_size(total_rows)
    block_count = total_rows // block_rows
    column_ids = jnp.arange(columns.shape[1], dtype=jnp.int32)

    def score_block(inputs):
        state_rows, wanted = inputs
        logits = jnp.dot(state_rows, columns, preferred_element_type=jnp.float32)
        maxima = jnp.max(logits, axis=1)
        weights = jnp.exp(logits - maxima[:, None])
        totals = jnp.sum(weights, axis=1)
        moments = jnp.sum(weights * logits, axis=1)
        picked = jnp.sum(jnp.where(column_ids[None, :] == wanted[:, None], logits, 0.0), axis=1)
        return (maxima, totals, moments, picked)

    results = lax.map(
        score_block,
        (
            states.reshape(block_count, block_rows, states.shape[1]),
            target_col.reshape(block_count, block_rows),
        ),
    )
    return tuple((member.reshape(total_rows) for member in results))


def body(hidden, norm_gain, head_weight, targets, lengths, prior_device, prior_row):
    row_count = hidden.shape[0]
    col_width = head_weight.shape[1]
    tok_index = lax.axis_index("tok")
    band_index = lax.axis_index("voc")
    voc_count = lax.axis_size("voc")
    asked_row = jnp.sum(jnp.where(prior_device == tok_index, prior_row, 0))
    outgoing = lax.dynamic_slice_in_dim(hidden, asked_row, 1, 0)
    incoming = lax.all_gather(outgoing, "tok", axis=0, tiled=True)
    source = select_entry(prior_device, tok_index)
    chosen = jnp.arange(incoming.shape[0], dtype=jnp.int32) == source
    fetched = jnp.sum(
        jnp.where(chosen[:, None], incoming.astype(jnp.float32), 0.0), axis=0, keepdims=True
    )
    scored = jnp.concatenate([fetched, hidden[:-1].astype(jnp.float32)], axis=0)
    normed = (
        scored
        * lax.rsqrt(jnp.mean(scored * scored, axis=1, keepdims=True) + epsilon)
        * norm_gain[None, :]
    ).astype(jnp.bfloat16)
    owner_block = targets // col_width
    target_col = jnp.where(
        owner_block % voc_count == band_index,
        owner_block // voc_count * col_width + targets % col_width,
        -1,
    )
    zeroes = jnp.zeros((row_count,), jnp.float32)
    initial = (jnp.full((row_count,), -1e30, jnp.float32), zeroes, zeroes, zeroes)
    maxima, totals, moments, picked = combine(
        initial,
        block_stats(normed, lax.all_gather(head_weight, "tok", axis=1, tiled=True), target_col),
    )
    largest = lax.pmax(maxima, "voc")
    factor = jnp.exp(maxima - largest)
    totals, moments, picked = lax.psum((totals * factor, moments * factor, picked), "voc")
    maxima = largest
    normalizer = maxima + jnp.log(totals)
    logprob = picked - normalizer
    entropy = normalizer - moments / totals
    live_count = select_entry(lengths, tok_index)
    valid = jnp.arange(row_count, dtype=jnp.int32) < live_count
    return (jnp.where(valid, logprob, 0.0), jnp.where(valid, entropy, 0.0))


def solution(mesh):
    in_specs = (P("tok", None), P(), P(None, ("tok", "voc")), P("tok"), P(), P(), P())
    out_specs = (P("tok"), P("tok"))
    return jax.shard_map(body, mesh=mesh, in_specs=in_specs, out_specs=out_specs, check_vma=False)
```

profile of v0, /device:TPU:1, one launch (start us, length us, event | category | flops | bytes accessed | tf_op | source)
XLA Modules:
  0.0 215.5 jit_solution(13861891363892837926)
XLA Ops:
  7.2 0.0 copy-start
  7.2 0.0 all-gather.3.cloned.1.call-start
  7.2 0.7 all-gather.3.cloned.1.call-update
  7.9 1.3 fusion.7
  11.2 0.8 dynamic-slice_bitcast_fusion
  11.9 42.7 %all-gather = bf16[32,1,1536]{2,1,0:T(2,128)(2,1)S(1)} all-gather(bf16[1,1,1536]{2,1,0:T(2,128)(2,1)S(1)} %dynamic-slice_bitcast_fusion), channel_id=1, replica_groups=mesh['tok'=32,'voc'=8] {'tok'}, dimensions={0}, use_global_device_ids=true | all-gather | bytes 101376 | tf_op jit(solution)/shard_map/all_gather | solution.py:61
  54.6 0.2 convert_element_type.12
  54.8 0.7 iota_compare_fusion.2
  55.5 0.1 fusion.4
  55.6 0.0 copy-done
  55.6 0.0 copy-start.3
  55.6 0.0 copy-start.1
  55.7 0.0 copy-start.2
  55.7 0.2 slice_convert_fusion
  55.8 0.3 multiply_reduce_fusion.1
  56.1 0.1 copy-done.3
  56.3 0.6 fusion.6
  56.9 0.0 copy-done.1
  57.0 108.5 %all-gather.3.cloned.1.call-done = bf16[1536,6144]{0,1:T(8,128)(2,1)} async-done(((bf16[1536,192]{0,1:T(8,128)(2,1)}), bf16[1536,6144]{0,1:T(8,128)(2,1)}) %all-gather.3.cloned.1.call-update) | async-done | bytes 18874384 | tf_op jit(solution)/shard_map/all_gather | solution.py:83
  165.4 0.0 copy-done.2
  165.4 10.8 %fusion.10 = (f32[256]{0:T(256)S(1)}, f32[256,6144]{1,0:T(8,128)}) fusion(bf16[1536,6144]{0,1:T(8,128)(2,1)} %all-gather.3.cloned.1.call-done, f32[255,1536]{1,0:T(8,128)S(1)} %slice_convert_fusion, f32[1,1536]{1,0:T(1,128)S(1)} %broadcast_in_dim.57, f32[1536]{0:T(1024)S(1)} %copy-done.2, f32[256]{0:T(256)S(1)} %add_rsqrt_fusion), kind=kOutput, calls=%fused_computation.42 | convolution fusion | flops 4834983936 | bytes 26746880 | tf_op jit(solution)/shard_map/while/body/eval_jaxpr/dot_general | solution.py:35
  176.3 12.8 %pmax.7 = f32[256]{0:T(256)S(1)} all-reduce(f32[256]{0:T(256)S(1)} %broadcast_maximum_fusion), channel_id=1, replica_groups=mesh['tok'=32,'voc'=8] {'voc'}, use_global_device_ids=true, to_apply=%region_8.9 | all-reduce | flops 256 | bytes 2048 | tf_op jit(solution)/shard_map/pmax | solution.py:85
  189.1 4.2 %multiply_reduce_fusion = (f32[256]{0:T(256)S(1)}, f32[256]{0:T(256)S(1)}, f32[256]{0:T(256)S(1)}) fusion(f32[256,6144]{1,0:T(8,128)} %get-tuple-element.42, f32[256]{0:T(256)S(1)} %get-tuple-element.41, s32[256]{0:T(256)S(1)} %compare_select_fusion.1), kind=kLoop, calls=%fused_computation | loop fusion | flops 11009280 | bytes 6296576 | tf_op jit(solution)/shard_map/while/body/eval_jaxpr/reduce_sum | solution.py:39
  193.2 14.2 %all-reduce = (f32[256]{0:T(256)S(1)}, f32[256]{0:T(256)S(1)}, f32[256]{0:T(256)S(1)}) all-reduce(f32[256]{0:T(256)S(1)} %get-tuple-element.22, f32[256]{0:T(256)S(1)} %get-tuple-element.40, f32[256]{0:T(256)S(1)} %get-tuple-element.39), channel_id=1, replica_groups=mesh['tok'=32,'voc'=8] {'voc'}, use_global_device_ids=true, to_apply=%region_6.7 | all-reduce | flops 768 | bytes 6144 | tf_op jit(solution)/shard_map/psum | solution.py:87
  207.4 1.2 subtract_select_fusion
  (5 shorter events, 0.1 us)
Async XLA Ops:
  7.2 48.5 %copy-start = (bf16[256,1536]{1,0:T(8,128)(2,1)S(1)}, bf16[256,1536]{1,0:T(8,128)(2,1)}, u32[]{:S(2)}) copy-start(bf16[256,1536]{1,0:T(8,128)(2,1)} %param.7) | copy-start | bytes 2359300
  7.2 158.2 %all-gather.3.cloned.1.call-start = ((), (), s32[]{:S(2)}) async-start(), calls=%async_computation | async-start | bytes 19464192 | tf_op jit(solution)/shard_map/all_gather | solution.py:83
  55.6 0.7 copy-start.3
  55.6 1.3 copy-start.1
  55.7 109.8 %copy-start.2 = (f32[1536]{0:T(1024)S(1)}, f32[1536]{0:T(1024)}, u32[]{:S(2)}) copy-start(f32[1536]{0:T(1024)} %param.8) | copy-start | bytes 18436
Sparse Core Ops, SparseCore 0:
  10.6 154.7 all-gather.2
where the time goes:
time: 216 us; the launch traced here: 215 us
  waiting for transfers between devices  109 us (50%)
  blocking collectives  69.7 us (32%)
  between operations  16.1 us (7%)
  matrix products  10.8 us (5%)
  other arithmetic  8.77 us (4%)
    all_gather x1, waiting for transfers between devices, body(): lax.all_gather(head_weight, 'tok', axis=1, tiled=True)  108 us
    all_gather x1, blocking collectives, body(): incoming = lax.all_gather(outgoing, 'tok', axis=0, tiled=True)  42.7 us
    psum x1, blocking collectives, body(): lax.psum((totals * factor, moments * factor, picked), 'voc')  14.2 us
    pmax x1, blocking collectives, body(): largest = lax.pmax(maxima, 'voc')  12.8 us
    dot_general x1, matrix products, score_block(): logits = jnp.dot(state_rows, columns, preferred_element_type=jnp.float32)  10.8 us
  transfers between devices with their start and end apart: 1, of which 1 were waited for; matrix products, arithmetic and copies ran while one was open for 2% of the time, Pallas kernels for 0%

commit v1 on v0

v1 whole, which is shorter than its diff:
```python
import jax
import jax.numpy as jnp
from jax import lax
from jax.experimental import pallas as pl
from jax.experimental.pallas import tpu as pltpu
from jax.sharding import PartitionSpec as P

epsilon = 1e-05
MESH = pl.DeviceIdType.MESH
NZ, NY, NX, NC = 8, 4, 4, 2
OFF = (0, -1, 1, -2, 2, -3, 3, 4)
MIRROR = (0, 2, 1, 4, 3, 6, 5, 7)
HALF, PIECE = 64, 32
LOWEST = -1e30


def message_numbers():
    names = ["own_s", "own_r0", "own_r1", "own_l0", "own_l1", "fwd_r", "fwd_l"]
    names += ["share_l0", "share_l1", "share_r0", "share_r1", "share_f0", "share_f1"]
    names += [("z", side, k, p) for side in "rl" for k in range(4) for p in range(2)]
    names += [("x", s, p) for s in range(1, NZ) for p in range(2)]
    names += [("target", s) for s in range(1, NZ)]
    names += [("row_y", d) for d in range(1, NY)]
    names += [("row_z", s) for s in range(1, NZ)]
    names += [("stat_z", s) for s in range(1, NZ)]
    names += [("stat_v", i, j) for i in range(NX) for j in range(NC) if i + j]
    return {name: at for at, name in enumerate(names)}


NUMBER = message_numbers()


def peer(dx=0, dy=0, dz=0, dc=0):
    tok, voc = lax.axis_index("tok"), lax.axis_index("voc")
    z, y, x, c = tok // NY, tok % NY, voc // NC, voc % NC
    return (
        ((z + dz + NZ) % NZ) * NY + (y + dy + NY) % NY,
        ((x + dx + NX) % NX) * NC + (c + dc) % NC,
    )


PEERS = (
    [dict(dy=d) for d in range(1, NY)]
    + [dict(dz=d) for d in range(1, NZ)]
    + [dict(dx=i, dc=j) for i in range(NX) for j in range(NC) if i + j]
)


def kernel(
    lengths, prior_device, prior_row, hidden, gain, weight, targets,
    logprob, entropy,
    wbuf, tbuf, gbuf, tgt, row_y, row_z, prior, stats, mine_z, got_z, mine_v, got_v,
    send, recv, local,
):
    tok, voc = lax.axis_index("tok"), lax.axis_index("voc")
    z, y, x, c = tok // NY, tok % NY, voc // NC, voc % NC
    kind = x % 2
    width = weight.shape[0]
    half = width // 2
    wide = 2 * width

    barrier = pltpu.get_barrier_semaphore()
    for offsets in PEERS:
        pl.semaphore_signal(barrier, inc=1, device_id=peer(**offsets), device_id_type=MESH)

    fetch = pltpu.make_async_copy(weight, wbuf.at[pl.ds(0, width)], local)
    fetch.start()

    def copy(name, source, target, **offsets):
        at = NUMBER[name]
        return pltpu.make_async_remote_copy(
            src_ref=source, dst_ref=target, send_sem=send.at[at], recv_sem=recv.at[at],
            device_id=peer(**offsets), device_id_type=MESH,
        )

    def wrows(start, rows):
        return wbuf.at[pl.ds(start, rows)]

    left, right, far = wide, 2 * wide, 3 * wide
    weight_messages = {
        "own_s": (0, width, width, dict(dc=1)),
        "own_r0": (0, left, half, dict(dy=1)),
        "own_r1": (half, left + half, half, dict(dy=1)),
        "own_l0": (0, right, half, dict(dy=-1)),
        "own_l1": (half, right + half, half, dict(dy=-1)),
        "fwd_r": (left, far, half, dict(dy=1)),
        "fwd_l": (right + half, far + half, half, dict(dy=-1)),
        "share_l0": (left, left + width, half, dict(dc=1)),
        "share_l1": (left + half, left + width + half, half, dict(dc=1)),
        "share_r0": (right, right + width, half, dict(dc=1)),
        "share_r1": (right + half, right + width + half, half, dict(dc=1)),
        "share_f0": (far, far + width, half, dict(dc=1)),
        "share_f1": (far + half, far + width + half, half, dict(dc=1)),
    }

    def weights(name):
        source, target, rows, offsets = weight_messages[name]
        return copy(name, wrows(source, rows), wrows(target, rows), **offsets)

    def trows(slot, which, p):
        start = pl.multiple_of(slot * 2 * HALF + which * HALF + p * PIECE, PIECE)
        return tbuf.at[pl.ds(start, PIECE)]

    source_slot = {"r": (0, 1, 3, 5), "l": (0, 2, 4, 6)}
    target_slot = {"r": (1, 3, 5, 7), "l": (2, 4, 6, 7)}

    def along_z(side, k, p):
        return copy(
            ("z", side, k, p),
            trows(source_slot[side][k], kind, p),
            trows(target_slot[side][k], kind, p),
            dz=1 if side == "r" else -1,
        )

    def along_x(s, p):
        return copy(("x", s, p), trows(s, kind, p), trows(s, kind, p), dx=1 if p == 0 else -1)

    def from_x(s, p):
        return copy(("x", s, p), trows(s, 1 - kind, p), trows(s, 1 - kind, p), dx=1 if p == 0 else -1)

    def target_message(s):
        return copy(("target", s), tgt.at[0], tgt.at[MIRROR[s]], dz=OFF[s])

    def target_arrival(s):
        return copy(("target", s), tgt.at[MIRROR[s]], tgt.at[MIRROR[s]], dz=OFF[s])

    def row_y_message(d):
        return copy(("row_y", d), row_y.at[0], row_y.at[d], dy=d)

    def row_z_message(s):
        return copy(("row_z", s), row_z.at[z], row_z.at[z], dz=OFF[s])

    def row_z_arrival(s):
        origin = (z - OFF[s] + NZ) % NZ
        return copy(("row_z", s), row_z.at[origin], row_z.at[origin], dz=OFF[s])

    def stat_z_message(s):
        return copy(("stat_z", s), mine_z.at[s], got_z.at[MIRROR[s]], dz=OFF[s])

    def stat_v_message(i, j):
        return copy(("stat_v", i, j), mine_v, got_v.at[voc], dx=i, dc=j)

    def stat_v_arrival(i, j):
        origin = ((x - i + NX) % NX) * NC + (c + j) % NC
        return copy(("stat_v", i, j), got_v.at[origin], got_v.at[origin], dx=i, dc=j)

    sent = []

    def start(make, *which):
        make(*which).start()
        sent.append((make, which))

    def norm(rows):
        mean = jnp.sum(rows * rows, axis=1, keepdims=True) / rows.shape[1]
        return rows * lax.rsqrt(mean + epsilon) * gain[...]

    mine = hidden[pl.ds(pl.multiple_of(c * 2 * HALF, 2 * HALF), 2 * HALF), :].astype(jnp.float32)
    tbuf[pl.ds(0, 2 * HALF), :] = norm(mine).astype(jnp.bfloat16)
    asked = jnp.int32(0)
    for t in range(NZ * NY):
        asked = asked + jnp.where(prior_device[t] == tok, prior_row[t], 0)
    shape = (8, hidden.shape[0])
    chosen = (lax.broadcasted_iota(jnp.int32, shape, 0) == y) & (lax.broadcasted_iota(jnp.int32, shape, 1) == asked)
    outgoing = jnp.dot(
        jnp.where(chosen, 1.0, 0.0).astype(jnp.bfloat16), hidden[...], preferred_element_type=jnp.float32
    )
    row_y[0] = norm(outgoing).astype(jnp.bfloat16)
    shifted = pltpu.roll(jnp.broadcast_to(targets[...], shape), shape[1] - 1, 1)
    tgt[0] = jnp.where(c == 0, shifted[:, : 2 * HALF], shifted[:, 2 * HALF :])
    prior[...] = jnp.zeros_like(prior)
    for g in range(4):
        stats[g, 0] = jnp.full(stats.shape[2:], LOWEST, jnp.float32)
        for k in range(1, 4):
            stats[g, k] = jnp.zeros(stats.shape[2:], jnp.float32)

    pl.semaphore_wait(barrier, len(PEERS))

    for d in range(1, NY):
        start(row_y_message, d)
    for p in range(2):
        start(along_z, "r", 0, p)
        start(along_z, "l", 0, 1 - p)
    fetch.wait()
    for name in ("own_r0", "own_l1", "own_r1", "own_l0", "own_s"):
        start(weights, name)
    for s in range(1, NZ):
        start(target_message, s)

    for d in range(1, NY):
        row_y_message(d).wait_recv()
    gathered = row_y[0].astype(jnp.float32)
    for d in range(1, NY):
        gathered = gathered + row_y[d].astype(jnp.float32)

    @pl.when(c == 1)
    def _():
        row_z[z] = gathered.astype(jnp.bfloat16)
        for s in range(1, NZ):
            row_z_message(s).start()

    def pass_on(k, late):
        for side in "rl":
            p = late if side == "r" else 1 - late
            slot = target_slot[side][k]
            along_z(side, k, p).wait_recv()
            if k < 2 or (k == 2 and late == 0):
                start(along_z, side, k + 1, p)
            start(along_x, slot, p)

    def whole(slot):
        for p in range(2):
            from_x(slot, p).wait_recv()

    def assemble(slots):
        for s in slots:
            low = s * 2 * HALF
            gbuf[low : low + 2 * HALF - 16] = tbuf[low : low + 2 * HALF - 16]
            last = tbuf[low + 2 * HALF - 16 : low + 2 * HALF].astype(jnp.float32)
            here = (lax.broadcasted_iota(jnp.int32, last.shape, 0) == 15) & (c == 1)
            last = jnp.where(here, jnp.broadcast_to(prior[s : s + 1, :], last.shape), last)
            gbuf[low + 2 * HALF - 16 : low + 2 * HALF] = last.astype(jnp.bfloat16)

    def unit(g, d):
        rows = 4 * HALF
        w = wbuf[pl.ds(pl.multiple_of(d * wide, wide), wide), :]
        t = gbuf[pl.ds(pl.multiple_of(g * rows, rows), rows), :]
        logits = lax.dot_general(w, t, (((1,), (1,)), ((), ())), preferred_element_type=jnp.float32)
        logits = logits.reshape(wide // 8, 8, rows)
        old = stats[g, 0]
        top = jnp.maximum(old, jnp.max(logits, axis=0))
        scale = jnp.exp(old - top)
        e = jnp.exp(logits - top[None])
        stats[g, 0] = top
        stats[g, 1] = stats[g, 1] * scale + jnp.sum(e, axis=0)
        stats[g, 2] = stats[g, 2] * scale + jnp.sum(e * logits, axis=0)
        y_of = (y + jnp.where(d == 1, 3, jnp.where(d == 2, 1, jnp.where(d == 3, 2, 0)))) % NY
        wanted = jnp.concatenate([tgt[2 * g], tgt[2 * g + 1]], axis=1) - lax.broadcasted_iota(jnp.int32, (8, rows), 0)
        picked = stats[g, 3]
        each = width // 8
        for s in range(NC):
            base = ((z * NY + y_of) * (NX * NC) + x * NC + (c + s) % NC) * width
            at = lax.broadcasted_iota(jnp.int32, (each, 8, rows), 0) * 8
            hit = at == (wanted - base)[None]
            picked = picked + jnp.sum(jnp.where(hit, logits[s * each : (s + 1) * each], 0.0), axis=0)
        stats[g, 3] = picked

    def first_units(k, carry):
        @pl.when(k == 0)
        def _():
            pass_on(0, 0)
            pass_on(0, 1)
            weights("own_r0").wait_recv()
            start(weights, "fwd_r")
            start(weights, "share_l0")
            weights("own_l1").wait_recv()
            start(weights, "fwd_l")
            start(weights, "share_r1")
            pass_on(1, 0)
            pass_on(1, 1)
            weights("own_s").wait_recv()
            for s in range(1, NZ):
                target_arrival(s).wait_recv()

            @pl.when(c == 1)
            def _():
                for s in range(1, NZ):
                    row_z_arrival(s).wait_recv()
                shape = (8, NZ * 8)
                wants = jnp.full(shape, -1, jnp.int32)
                sub = lax.broadcasted_iota(jnp.int32, shape, 0)
                for s in range(NZ):
                    turn = ((z + OFF[s] + NZ) % NZ) * NY + y
                    wants = jnp.where(sub == s, prior_device[turn], wants)
                lane = lax.broadcasted_iota(jnp.int32, shape, 1)
                block = jnp.where(lane % 8 < NY, lane // 8 * NY + lane % 8, -2)
                pick = jnp.where(wants == block, 1.0, 0.0).astype(jnp.bfloat16)
                table = row_z[...].reshape(NZ * 8, row_z.shape[2])
                prior[...] = jnp.dot(pick, table, preferred_element_type=jnp.float32)

            whole(1)
            assemble((0, 1))

        @pl.when(k == 1)
        def _():
            pass_on(2, 0)
            weights("own_r1").wait_recv()
            start(weights, "share_l1")
            weights("own_l0").wait_recv()
            start(weights, "share_r0")
            pass_on(2, 1)
            for name in ("share_l0", "share_l1", "share_r0", "share_r1"):
                weights(name).wait_recv()

        @pl.when(k == 3)
        def _():
            whole(2)
            whole(3)
            assemble((2, 3))

        @pl.when(k == 6)
        def _():
            along_z("r", 3, 0).wait_recv()
            start(along_x, 7, 0)
            along_z("l", 3, 1).wait_recv()
            start(along_x, 7, 1)
            whole(4)
            whole(5)
            assemble((4, 5))

        @pl.when(k == 9)
        def _():
            weights("fwd_r").wait_recv()
            start(weights, "share_f0")
            weights("fwd_l").wait_recv()
            start(weights, "share_f1")
            whole(6)
            whole(7)
            assemble((6, 7))

        @pl.when(k == 12)
        def _():
            weights("share_f0").wait_recv()
            weights("share_f1").wait_recv()

        unit(jnp.where(k < 12, k // 3, k - 12), jnp.where(k < 12, k % 3, 3))
        return carry

    lax.fori_loop(0, 16, first_units, 0)

    sub = lax.broadcasted_iota(jnp.int32, (8, 2 * HALF), 0)

    def tile(top, total, moment, picked):
        return jnp.where(sub == 0, top, jnp.where(sub == 1, total, jnp.where(sub == 2, moment, picked)))

    for s in range(NZ):
        lanes = slice(s % 2 * 2 * HALF, (s % 2 + 1) * 2 * HALF)
        tops = stats[s // 2, 0, :, lanes]
        top = jnp.max(tops, axis=0, keepdims=True)
        scale = jnp.exp(tops - top)
        total = jnp.sum(stats[s // 2, 1, :, lanes] * scale, axis=0, keepdims=True)
        moment = jnp.sum(stats[s // 2, 2, :, lanes] * scale, axis=0, keepdims=True)
        picked = jnp.sum(stats[s // 2, 3, :, lanes], axis=0, keepdims=True)
        mine_z[s] = tile(top, total, moment, picked)
        if s:
            start(stat_z_message, s)

    def merge(tiles):
        top = tiles[0][0:1]
        for other in tiles[1:]:
            top = jnp.maximum(top, other[0:1])
        total, moment, picked = 0.0, 0.0, 0.0
        for one in tiles:
            scale = jnp.exp(one[0:1] - top)
            total = total + one[1:2] * scale
            moment = moment + one[2:3] * scale
            picked = picked + one[3:4]
        return top, total, moment, picked

    for s in range(1, NZ):
        copy(("stat_z", s), mine_z.at[s], got_z.at[MIRROR[s]], dz=OFF[s]).wait_recv()
    merged = tile(*merge([mine_z[0]] + [got_z[s] for s in range(1, NZ)]))
    mine_v[...] = merged
    for i in range(NX):
        for j in range(NC):
            if i + j:
                start(stat_v_message, i, j)
    got_v[voc] = merged
    for i in range(NX):
        for j in range(NC):
            if i + j:
                stat_v_arrival(i, j).wait_recv()
    row_of, entropy_of = [], []
    for h in range(NC):
        top, total, moment, picked = merge([got_v[i * NC + h] for i in range(NX)])
        normalizer = top + jnp.log(total)
        row_of.append(picked - normalizer)
        entropy_of.append(normalizer - moment / total)
    live = lax.broadcasted_iota(jnp.int32, (1, 4 * HALF), 1) < lengths[tok]

    def finished(parts):
        both = jnp.broadcast_to(jnp.concatenate(parts, axis=1), (8, 4 * HALF))
        return jnp.where(live, pltpu.roll(both, 1, 1)[0:1], 0.0)

    logprob[...] = finished(row_of)
    entropy[...] = finished(entropy_of)

    for make, which in sent:
        make(*which).wait_send()

    @pl.when(c == 1)
    def _():
        for s in range(1, NZ):
            row_z_message(s).wait_send()


def body(hidden, norm_gain, head_weight, targets, lengths, prior_device, prior_row):
    rows, features = hidden.shape
    width = head_weight.shape[1]
    vmem, smem = pl.BlockSpec(memory_space=pltpu.VMEM), pl.BlockSpec(memory_space=pltpu.SMEM)
    f32, bf16 = jnp.float32, jnp.bfloat16
    out = jax.ShapeDtypeStruct((1, rows), f32)
    lanes = 2 * HALF
    logprob, entropy = pl.pallas_call(
        kernel,
        out_shape=(out, out),
        in_specs=[smem, smem, smem, vmem, vmem, pl.BlockSpec(memory_space=pl.ANY), vmem],
        out_specs=(vmem, vmem),
        scratch_shapes=[
            pltpu.VMEM((8 * width, features), bf16),
            pltpu.VMEM((NZ * lanes, features), bf16),
            pltpu.VMEM((NZ * lanes, features), bf16),
            pltpu.VMEM((NZ, 8, lanes), jnp.int32),
            pltpu.VMEM((NY, 8, features), bf16),
            pltpu.VMEM((NZ, 8, features), bf16),
            pltpu.VMEM((8, features), f32),
            pltpu.VMEM((4, 4, 8, 2 * lanes), f32),
            pltpu.VMEM((NZ, 8, lanes), f32),
            pltpu.VMEM((NZ, 8, lanes), f32),
            pltpu.VMEM((8, lanes), f32),
            pltpu.VMEM((NX * NC, 8, lanes), f32),
            pltpu.SemaphoreType.DMA((len(NUMBER),)),
            pltpu.SemaphoreType.DMA((len(NUMBER),)),
            pltpu.SemaphoreType.DMA,
        ],
        compiler_params=pltpu.CompilerParams(
            collective_id=0, has_side_effects=True, vmem_limit_bytes=48 * 2**20
        ),
    )(
        lengths, prior_device, prior_row, hidden, norm_gain.reshape(1, features), head_weight.T,
        targets.reshape(1, rows),
    )
    return logprob.reshape(rows), entropy.reshape(rows)


def solution(mesh):
    in_specs = (P("tok", None), P(), P(None, ("tok", "voc")), P("tok"), P(), P(), P())
    out_specs = (P("tok"), P("tok"))
    return jax.shard_map(body, mesh=mesh, in_specs=in_specs, out_specs=out_specs, check_vma=False)
```

time: 216 us -> 56.6 us (0.26)
  waiting for transfers between devices: 109 us -> 0 us
  blocking collectives: 69.7 us -> 0 us
  Pallas kernels: 0 us -> 51.7 us
  between operations: 16.1 us -> 0.7 us
  matrix products: 10.8 us -> 0 us
  other arithmetic: 8.77 us -> 0 us
  local copies, waits for them, and re-layouts: 0.93 us -> 4.06 us
    all_gather x1 -> x0, waiting for transfers between devices: 108 us -> none  [body(): lax.all_gather(head_weight, 'tok', axis=1, tiled=True)]
    pallas_call x0 -> x1, Pallas kernels: none -> 51.7 us  [body(): pl.pallas_call(kernel, out_shape=(out, out), in_specs=[smem, smem, smem,...]
    all_gather x1 -> x0, blocking collectives: 42.7 us -> none  [body(): incoming = lax.all_gather(outgoing, 'tok', axis=0, tiled=True)]
    psum x1 -> x0, blocking collectives: 14.2 us -> none  [body(): lax.psum((totals * factor, moments * factor, picked), 'voc')]
    pmax x1 -> x0, blocking collectives: 12.8 us -> none  [body(): largest = lax.pmax(maxima, 'voc')]
    dot_general x1 -> x0, matrix products: 10.8 us -> none  [score_block(): logits = jnp.dot(state_rows, columns, preferred_element_type=jnp.float32)]
    reduce_sum x5 -> x0, other arithmetic: 6.5 us -> none  [the longest x1 4.16 us: score_block(): moments = jnp.sum(weights * logits, axis=1)]
    unnamed x9 -> x14, local copies, waits for them, and re-layouts: 0.92 us -> 3.34 us
  transfers between devices with their start and end apart: 1 -> 0, of which waited for: 1 -> 0; matrix products, arithmetic and copies ran while one was open for 2% -> 0% of each run, Pallas kernels for 0% -> 0%
where the time goes in v1:
time: 56.6 us; the launch traced here: 56.4 us
  Pallas kernels  51.7 us (91%)
  local copies, waits for them, and re-layouts  4.06 us (7%)
  between operations  0.7 us (1%)
    pallas_call x1, Pallas kernels, body(): pl.pallas_call(kernel, out_shape=(out, out), in_specs=[smem, smem, smem,...  51.7 us
    unnamed x14, local copies, waits for them, and re-layouts  3.34 us

profile of v1, /device:TPU:1, one launch (start us, length us, event | category | flops | bytes accessed | tf_op | source)
XLA Modules:
  0.0 56.4 jit_solution(15030769102848546529)
XLA Ops:
  0.6 0.0 copy-start.2
  0.6 0.0 copy-start.3
  0.7 0.0 copy-start.4
  0.7 0.0 copy-start.5
  0.7 0.7 %reshape.16.gain = f32[1,1536]{1,0:T(1,128)S(1)} reshape(f32[1536]{0:T(1024)} %param.8) | data formatting | bytes 12288 | tf_op jit(solution)/shard_map/reshape | solution.py:429
  1.4 0.0 copy-done.2
  1.4 0.0 copy-done.3
  1.4 0.0 copy-done.4
  1.4 0.0 copy-done.5
  1.4 0.0 copy-start
  1.4 1.1 %copy-done = bf16[256,1536]{1,0:T(8,128)(2,1)S(1)} copy-done((bf16[256,1536]{1,0:T(8,128)(2,1)S(1)}, bf16[256,1536]{1,0:T(8,128)(2,1)}, u32[]{:S(2)}) %copy-start) | copy-done | bytes 786456
  2.6 0.0 copy-start.1
  2.6 1.1 %copy-done.1 = bf16[1536,192]{0,1:T(8,128)(2,1)S(1)} copy-done((bf16[1536,192]{0,1:T(8,128)(2,1)S(1)}, bf16[1536,192]{0,1:T(8,128)(2,1)}, u32[]{:S(2)}) %copy-start.1) | copy-done | bytes 589848
  3.6 51.7 %shard_map.86 = (f32[1,256]{1,0:T(1,128)S(1)}, f32[1,256]{1,0:T(1,128)S(1)}) custom-call(s32[32]{0:T(128)S(1)} %copy-done.3, s32[32]{0:T(128)S(1)} %copy-done.4, s32[32]{0:T(128)S(1)} %copy-done.5, bf16[256,1536]{1,0:T(8,128)(2,1)S(1)} %copy-done, f32[1,1536]{1,0:T(1,128)S(1)} %reshape.16.gain, bf16[192,1536]{1,0:T(8,128)(2,1)S(1)} %bitcast.4, ...), custom_call_target="tpu_custom_call" | custom-call | tf_op jit(solution)/shard_map/pallas_call | solution.py:403
  55.3 0.6 %copy.11 = f32[256]{0:T(256)} copy(f32[256]{0:T(256)S(1)} %bitcast.7) | data formatting | bytes 2048
  55.9 0.6 copy.12
Async XLA Ops:
  0.6 0.8 %copy-start.2 = (s32[256]{0:T(256)S(1)}, s32[256]{0:T(256)}, u32[]{:S(2)}) copy-start(s32[256]{0:T(256)} %param.10) | copy-start | bytes 3076
  0.6 0.8 %copy-start.3 = (s32[32]{0:T(128)S(1)}, s32[32]{0:T(128)}, u32[]{:S(2)}) copy-start(s32[32]{0:T(128)} %lengths.1) | copy-start | bytes 388
  0.7 0.8 %copy-start.4 = (s32[32]{0:T(128)S(1)}, s32[32]{0:T(128)}, u32[]{:S(2)}) copy-start(s32[32]{0:T(128)} %prior_device.1) | copy-start | bytes 388
  0.7 0.8 %copy-start.5 = (s32[32]{0:T(128)S(1)}, s32[32]{0:T(128)}, u32[]{:S(2)}) copy-start(s32[32]{0:T(128)} %prior_row.1) | copy-start | bytes 388
  1.4 1.1 %copy-start = (bf16[256,1536]{1,0:T(8,128)(2,1)S(1)}, bf16[256,1536]{1,0:T(8,128)(2,1)}, u32[]{:S(2)}) copy-start(bf16[256,1536]{1,0:T(8,128)(2,1)} %hidden.1) | copy-start | bytes 2359300
  2.6 1.1 %copy-start.1 = (bf16[1536,192]{0,1:T(8,128)(2,1)S(1)}, bf16[1536,192]{0,1:T(8,128)(2,1)}, u32[]{:S(2)}) copy-start(bf16[1536,192]{0,1:T(8,128)(2,1)} %param.9) | copy-start | bytes 1769476

commit v2 on v1

v2 whole, which is shorter than its diff:
```python
import jax
import jax.numpy as jnp
from jax import lax
from jax.experimental import pallas as pl
from jax.experimental.pallas import tpu as pltpu
from jax.sharding import PartitionSpec as P

epsilon = 1e-05
MESH = pl.DeviceIdType.MESH
NZ, NY, NX, NC = 8, 4, 4, 2
OFF = (0, -1, 1, -2, 2, -3, 3, 4)
MIRROR = (0, 2, 1, 4, 3, 6, 5, 7)
HALF, PIECE = 64, 32
KEPT = (None, 128, 192, 384, 448, 640, 704, 896)
SWAPPED = (None, 256, 320, 512, 576, 768, 832, 960)
LOWEST = -1e30


def message_numbers():
    names = ["own_s"] + [(side, part) for side in "rl" for part in ("a", "b", "f0", "f1", "f2")]
    names += [("share", d, q) for d in range(1, 3) for q in (0, 2)]
    names += [("share", 3, q, step) for q in (0, 2) for step in range(3)]
    names += [("z", side, k, p) for side in "rl" for k in range(4) for p in range(2)]
    names += [("x", s, p) for s in range(1, NZ) for p in range(2)]
    names += [("target", s) for s in range(1, NZ)]
    names += [("row_y", d) for d in range(1, NY)]
    names += [("row_z", s) for s in range(1, NZ)]
    names += [("stat_z", s) for s in range(1, NZ)]
    names += [("stat_v", i, j) for i in range(NX) for j in range(NC) if i + j]
    return {name: at for at, name in enumerate(names)}


NUMBER = message_numbers()


def peer(dx=0, dy=0, dz=0, dc=0):
    tok, voc = lax.axis_index("tok"), lax.axis_index("voc")
    z, y, x, c = tok // NY, tok % NY, voc // NC, voc % NC
    return (
        ((z + dz + NZ) % NZ) * NY + (y + dy + NY) % NY,
        ((x + dx + NX) % NX) * NC + (c + dc) % NC,
    )


PEERS = [dict(dx=1), dict(dx=-1), dict(dz=1), dict(dz=-1), dict(dc=1)] + [dict(dy=d) for d in range(1, NY)]
RELAYS = 4


def kernel(
    lengths_hbm, device_hbm, row_hbm, hidden_hbm, gain_hbm, weight, targets_hbm,
    logprob, entropy,
    lengths, prior_device, prior_row, hidden, gain, targets,
    wbuf, tbuf, gbuf, tgt, wanted, row_y, row_z, prior, stats, mine_z, got_z, mine_v, got_v,
    send, recv, local, relay,
):
    tok, voc = lax.axis_index("tok"), lax.axis_index("voc")
    z, y, x, c = tok // NY, tok % NY, voc // NC, voc % NC
    kind = x % 2
    width = weight.shape[0]
    half = width // 2
    third = half // 3
    wide = 2 * width
    block = 2 * HALF

    own_rows = pl.ds(pl.multiple_of(c * block, block), block)
    other_rows = pl.ds(pl.multiple_of((1 - c) * block, block), block)
    fetches = [
        pltpu.make_async_copy(weight, wbuf.at[pl.ds(0, width)], local.at[0]),
        pltpu.make_async_copy(hidden_hbm.at[own_rows], hidden.at[own_rows], local.at[1]),
        pltpu.make_async_copy(gain_hbm, gain, local.at[2]),
        pltpu.make_async_copy(hidden_hbm.at[other_rows], hidden.at[other_rows], local.at[3]),
        pltpu.make_async_copy(device_hbm, prior_device, local.at[4]),
        pltpu.make_async_copy(row_hbm, prior_row, local.at[5]),
        pltpu.make_async_copy(targets_hbm, targets, local.at[6]),
        pltpu.make_async_copy(lengths_hbm, lengths, local.at[7]),
    ]
    barrier = pltpu.get_barrier_semaphore()
    for offsets in PEERS:
        pl.semaphore_signal(barrier, inc=1, device_id=peer(**offsets), device_id_type=MESH)
    for fetch in fetches:
        fetch.start()

    def copy(name, source, target, **offsets):
        at = NUMBER[name]
        return pltpu.make_async_remote_copy(
            src_ref=source, dst_ref=target, send_sem=send.at[at], recv_sem=recv.at[at],
            device_id=peer(**offsets), device_id_type=MESH,
        )

    def part_row(d, q):
        return d * wide + q * half

    def weights(name):
        if name == "own_s":
            source, target, rows, offsets = 0, width, width, dict(dc=1)
        elif name[0] == "share" and name[1] == 3:
            step = name[3] * third
            source, target, rows = part_row(3, name[2]) + step, part_row(3, name[2] + 1) + step, third
            offsets = dict(dc=1)
        elif name[0] == "share":
            source, target, rows = part_row(name[1], name[2]), part_row(name[1], name[2] + 1), half
            offsets = dict(dc=1)
        else:
            side, part = name
            q, offsets = (0, dict(dy=1)) if side == "r" else (2, dict(dy=-1))
            first = 0 if side == "r" else half
            if part == "b":
                source, target, rows = half - first, part_row(2, q), half
            elif part == "a":
                source, target, rows = first, part_row(1, q), half
            else:
                step = int(part[1]) * third
                source, target, rows = part_row(1, q) + step, part_row(3, q) + step, third
        return copy(name, wbuf.at[pl.ds(source, rows)], wbuf.at[pl.ds(target, rows)], **offsets)

    source_slot = {"r": (0, 1, 3, 5), "l": (0, 2, 4, 6)}
    target_slot = {"r": (1, 3, 5, 7), "l": (2, 4, 6, 7)}

    def piece(start, p):
        return tbuf.at[pl.ds(start + p * PIECE, PIECE)]

    def along_z(side, k, p):
        if k:
            source = piece(KEPT[source_slot[side][k]], p)
        else:
            source = tbuf.at[pl.ds(pl.multiple_of(kind * HALF + p * PIECE, PIECE), PIECE)]
        return copy(
            ("z", side, k, p), source, piece(KEPT[target_slot[side][k]], p), dz=1 if side == "r" else -1
        )

    def along_x(s, p):
        return copy(("x", s, p), piece(KEPT[s], p), piece(SWAPPED[s], p), dx=1 if p == 0 else -1)

    def target_message(s):
        return copy(("target", s), tgt.at[0], tgt.at[MIRROR[s]], dz=OFF[s])

    def row_y_message(d):
        return copy(("row_y", d), row_y.at[0], row_y.at[d], dy=d)

    def row_z_message(s):
        return copy(("row_z", s), row_z.at[z], row_z.at[z], dz=OFF[s])

    def row_z_arrival(s):
        origin = (z - OFF[s] + NZ) % NZ
        return copy(("row_z", s), row_z.at[origin], row_z.at[origin], dz=OFF[s])

    def stat_z_message(s):
        return copy(("stat_z", s), mine_z.at[s], got_z.at[MIRROR[s]], dz=OFF[s])

    def stat_v_message(i, j):
        return copy(("stat_v", i, j), mine_v, got_v.at[voc], dx=i, dc=j)

    def stat_v_arrival(i, j):
        origin = ((x - i + NX) % NX) * NC + (c + j) % NC
        return copy(("stat_v", i, j), got_v.at[origin], got_v.at[origin], dx=i, dc=j)

    sent = []

    def start(make, *which):
        make(*which).start()
        sent.append((make, which))

    def norm(rows):
        mean = jnp.sum(rows * rows, axis=1, keepdims=True) / rows.shape[1]
        return rows * lax.rsqrt(mean + epsilon) * gain[...]

    def norm_half(which):
        low = pl.multiple_of(c * block + which * HALF, HALF)
        rows = norm(hidden[pl.ds(low, HALF), :].astype(jnp.float32))
        tbuf[pl.ds(pl.multiple_of(which * HALF, HALF), HALF), :] = rows.astype(jnp.bfloat16)

    for fetch in fetches[1:]:
        fetch.wait()
    norm_half(kind)
    asked = jnp.int32(0)
    for t in range(NZ * NY):
        asked = asked + jnp.where(prior_device[t] == tok, prior_row[t], 0)
    shape = (8, hidden.shape[0])
    chosen = (lax.broadcasted_iota(jnp.int32, shape, 0) == y) & (lax.broadcasted_iota(jnp.int32, shape, 1) == asked)
    outgoing = jnp.dot(
        jnp.where(chosen, 1.0, 0.0).astype(jnp.bfloat16), hidden[...], preferred_element_type=jnp.float32
    )
    row_y[0] = norm(outgoing).astype(jnp.bfloat16)
    fetches[0].wait()

    pl.semaphore_wait(barrier, len(PEERS))
    for d in range(1, NY):
        start(row_y_message, d)
    for p in range(2):
        start(along_z, "r", 0, p)
        start(along_z, "l", 0, 1 - p)
    for part in "ab":
        for side in "rl":
            start(weights, (side, part))
    start(weights, "own_s")

    def tell(level, axis):
        for d in (1, -1):
            pl.semaphore_signal(relay.at[level], inc=1, device_id=peer(**{axis: d}), device_id_type=MESH)

    tell(0, "dz")
    tell(3, "dx")

    def turned(value):
        return jnp.where(kind == 0, value, pltpu.roll(value, HALF, 1))

    shifted = pltpu.roll(jnp.broadcast_to(targets[...], shape), shape[1] - 1, 1)
    straight = jnp.where(c == 0, shifted[:, :block], shifted[:, block:])
    tgt[0] = turned(straight)
    pl.semaphore_wait(relay.at[0], 2)
    tell(1, "dz")
    norm_half(1 - kind)
    prior[...] = jnp.zeros_like(prior)
    for g in range(4):
        stats[g, 0] = jnp.full(stats.shape[2:], LOWEST, jnp.float32)
        for k in range(1, 4):
            stats[g, k] = jnp.zeros(stats.shape[2:], jnp.float32)
    pl.semaphore_wait(relay.at[1], 2)
    tell(2, "dz")
    pl.semaphore_wait(relay.at[3], 2)
    for d in range(1, NY):
        row_y_message(d).wait_recv()
    gathered = row_y[0].astype(jnp.float32)
    for d in range(1, NY):
        gathered = gathered + row_y[d].astype(jnp.float32)
    pl.semaphore_wait(relay.at[2], 2)

    @pl.when(c == 1)
    def _():
        row_z[z] = gathered[:NY].astype(jnp.bfloat16)
        for s in range(1, NZ):
            row_z_message(s).start()

    for s in range(1, NZ):
        start(target_message, s)

    def pass_on(k, late):
        for side in "rl":
            p = late if side == "r" else 1 - late
            along_z(side, k, p).wait_recv()
            if k < 2 or (k == 2 and late == 0):
                start(along_z, side, k + 1, p)
            start(along_x, target_slot[side][k], p)

    def whole(slot):
        for p in range(2):
            along_x(slot, p).wait_recv()

    def assemble(g):
        rows = 2 * block
        gbuf[g * rows : (g + 1) * rows] = tbuf[g * rows : (g + 1) * rows]
        tails = [(HALF, 0, 1)] if g == 0 else []
        tails += [(KEPT[s], s, kind) for s in range(1, NZ)] + [(SWAPPED[s], s, 1 - kind) for s in range(1, NZ)]
        for low, s, which in tails:
            if low // rows == g:
                last = tbuf[low + HALF - 16 : low + HALF].astype(jnp.float32)
                here = (lax.broadcasted_iota(jnp.int32, last.shape, 0) == 15) & (c * which == 1)
                last = jnp.where(here, jnp.broadcast_to(prior[s : s + 1, :], last.shape), last)
                gbuf[low + HALF - 16 : low + HALF] = last.astype(jnp.bfloat16)

    lane = lax.broadcasted_iota(jnp.int32, (8, block), 1)

    def kept_pair(first, second):
        return jnp.where(lane < HALF, first, pltpu.roll(second, HALF, 1))

    def swapped_pair(first, second):
        return jnp.where(lane < HALF, pltpu.roll(first, HALF, 1), second)

    def unit(g, d):
        rows = 2 * block
        w = wbuf[pl.ds(pl.multiple_of(d * wide, wide), wide), :]
        t = gbuf[pl.ds(pl.multiple_of(g * rows, rows), rows), :]
        logits = lax.dot_general(w, t, (((1,), (1,)), ((), ())), preferred_element_type=jnp.float32)
        logits = logits.reshape(wide // 8, 8, rows)
        old = stats[g, 0]
        top = jnp.maximum(old, jnp.max(logits, axis=0))
        scale = jnp.exp(old - top)
        e = jnp.exp(logits - top[None])
        stats[g, 0] = top
        stats[g, 1] = stats[g, 1] * scale + jnp.sum(e, axis=0)
        stats[g, 2] = stats[g, 2] * scale + jnp.sum(e * logits, axis=0)
        picked = stats[g, 3]
        each = half // 8
        for q in range(4):
            side = jnp.where(d == 0, 0, jnp.where(d == 3, 2, 3 if q < 2 else 1))
            core = jnp.where(d == 0, q // 2, q % 2)
            part = jnp.where(d == 0, q % 2, jnp.where(d == 2, 1 - q // 2, q // 2))
            device = (z * NY + (y + side) % NY) * (NX * NC) + x * NC + (c + core) % NC
            at = lax.broadcasted_iota(jnp.int32, (each, 8, rows), 0) * 8
            hit = at == (wanted[g] - (device * width + part * half))[None]
            picked = picked + jnp.sum(jnp.where(hit, logits[q * each : (q + 1) * each], 0.0), axis=0)
        stats[g, 3] = picked

    sub = lax.broadcasted_iota(jnp.int32, (8, block), 0)

    def tile(top, total, moment, picked):
        return jnp.where(sub == 0, top, jnp.where(sub == 1, total, jnp.where(sub == 2, moment, picked)))

    def reduced(g, which):
        lanes = slice(which * block, (which + 1) * block)
        tops = stats[g, 0, :, lanes]
        top = jnp.max(tops, axis=0, keepdims=True)
        scale = jnp.exp(tops - top)
        return tile(
            top,
            jnp.sum(stats[g, 1, :, lanes] * scale, axis=0, keepdims=True),
            jnp.sum(stats[g, 2, :, lanes] * scale, axis=0, keepdims=True),
            jnp.sum(stats[g, 3, :, lanes], axis=0, keepdims=True),
        )

    def give_pair(g):
        kept, swapped = reduced(g, 1), reduced(g + 1, 0)
        mine_z[2 * g + 1] = kept_pair(kept, swapped)
        mine_z[2 * g + 2] = jnp.where(lane < HALF, pltpu.roll(kept, HALF, 1), swapped)

    def units(k, carry):
        @pl.when(k == 0)
        def _():
            pass_on(0, 0)
            pass_on(0, 1)
            for q, side in ((0, "r"), (2, "l")):
                weights((side, "a")).wait_recv()
                for step in range(3):
                    start(weights, (side, f"f{step}"))
                start(weights, ("share", 1, q))
            pass_on(1, 0)
            pass_on(1, 1)
            weights("own_s").wait_recv()
            for s in range(1, NZ):
                target_message(s).wait_recv()
            pairs = [(s, s + 1) for s in (1, 3, 5)]
            kept = [kept_pair(tgt[i], tgt[j]) for i, j in pairs]
            swapped = [swapped_pair(tgt[i], tgt[j]) for i, j in pairs]
            for g, both in enumerate(zip([straight] + swapped, kept + [tgt[7]])):
                place = lax.broadcasted_iota(jnp.int32, (8, 2 * block), 0)
                wanted[g] = jnp.concatenate(both, axis=1) - place

            @pl.when(c == 1)
            def _():
                for s in range(1, NZ):
                    row_z_arrival(s).wait_recv()
                shape = (8, NZ * NY)
                wants = jnp.full(shape, -1, jnp.int32)
                place = lax.broadcasted_iota(jnp.int32, shape, 0)
                for s in range(NZ):
                    turn = ((z + OFF[s] + NZ) % NZ) * NY + y
                    wants = jnp.where(place == s, prior_device[turn], wants)
                across = lax.broadcasted_iota(jnp.int32, shape, 1)
                pick = jnp.where(wants == across, 1.0, 0.0).astype(jnp.bfloat16)
                table = row_z[...].reshape(NZ * NY, row_z.shape[2])
                prior[...] = jnp.dot(pick, table, preferred_element_type=jnp.float32)

            whole(1)
            whole(2)
            assemble(0)
            assemble(1)

        @pl.when(k == 2)
        def _():
            pass_on(2, 0)
            weights(("share", 1, 0)).wait_recv()
            weights(("share", 1, 2)).wait_recv()

        @pl.when(k == 4)
        def _():
            pass_on(2, 1)
            for q, side in ((0, "r"), (2, "l")):
                weights((side, "b")).wait_recv()
                start(weights, ("share", 2, q))
            whole(3)
            whole(4)
            assemble(2)

        def share_far(step):
            for q, side in ((0, "r"), (2, "l")):
                weights((side, f"f{step}")).wait_recv()
                start(weights, ("share", 3, q, step))

        @pl.when(k == 6)
        def _():
            along_z("r", 3, 0).wait_recv()
            start(along_x, 7, 0)
            along_z("l", 3, 1).wait_recv()
            start(along_x, 7, 1)
            share_far(0)
            for q in (0, 2):
                weights(("share", 2, q)).wait_recv()

        @pl.when(k == 8)
        def _():
            share_far(1)

        @pl.when(k == 9)
        def _():
            whole(5)
            whole(6)
            whole(7)
            assemble(3)

        @pl.when(k == 10)
        def _():
            share_far(2)

        @pl.when(k == 12)
        def _():
            for q in (0, 2):
                for step in range(3):
                    weights(("share", 3, q, step)).wait_recv()

        @pl.when(k == 13)
        def _():
            mine_z[7] = reduced(3, 1)
            start(stat_z_message, 7)

        @pl.when(k == 14)
        def _():
            give_pair(2)
            start(stat_z_message, 5)
            start(stat_z_message, 6)

        @pl.when(k == 15)
        def _():
            give_pair(1)
            start(stat_z_message, 3)
            start(stat_z_message, 4)

        early = jnp.where(k < 4, k % 2, jnp.where(k < 6, 2, k - 6))
        unit(
            jnp.where(k < 9, early, jnp.where(k < 12, 3, 15 - k)),
            jnp.where(k < 4, k // 2, jnp.where(k < 6, k - 4, jnp.where(k < 9, 2, jnp.where(k < 12, k - 9, 3)))),
        )
        return carry

    lax.fori_loop(0, 16, units, 0)
    give_pair(0)
    start(stat_z_message, 1)
    start(stat_z_message, 2)
    mine_z[0] = turned(reduced(0, 0))

    def merge(tiles):
        top = tiles[0][0:1]
        for other in tiles[1:]:
            top = jnp.maximum(top, other[0:1])
        total, moment, picked = 0.0, 0.0, 0.0
        for one in tiles:
            scale = jnp.exp(one[0:1] - top)
            total = total + one[1:2] * scale
            moment = moment + one[2:3] * scale
            picked = picked + one[3:4]
        return top, total, moment, picked

    for s in range(1, NZ):
        stat_z_message(s).wait_recv()
    merged = turned(tile(*merge([mine_z[0]] + [got_z[s] for s in range(1, NZ)])))
    mine_v[...] = merged
    for i in range(NX):
        for j in range(NC):
            if i + j:
                start(stat_v_message, i, j)
    got_v[voc] = merged
    for i in range(NX):
        for j in range(NC):
            if i + j:
                stat_v_arrival(i, j).wait_recv()
    row_of, entropy_of = [], []
    for h in range(NC):
        top, total, moment, picked = merge([got_v[i * NC + h] for i in range(NX)])
        normalizer = top + jnp.log(total)
        row_of.append(picked - normalizer)
        entropy_of.append(normalizer - moment / total)
    live = lax.broadcasted_iota(jnp.int32, (1, 2 * block), 1) < lengths[tok]

    def finished(parts):
        both = jnp.broadcast_to(jnp.concatenate(parts, axis=1), (8, 2 * block))
        return jnp.where(live, pltpu.roll(both, 1, 1)[0:1], 0.0)

    logprob[...] = finished(row_of)
    entropy[...] = finished(entropy_of)

    for make, which in sent:
        make(*which).wait_send()

    @pl.when(c == 1)
    def _():
        for s in range(1, NZ):
            row_z_message(s).wait_send()


def body(hidden, norm_gain, head_weight, targets, lengths, prior_device, prior_row):
    rows, features = hidden.shape
    width = head_weight.shape[1]
    vmem, hbm = pl.BlockSpec(memory_space=pltpu.VMEM), pl.BlockSpec(memory_space=pltpu.HBM)
    f32, bf16 = jnp.float32, jnp.bfloat16
    out = jax.ShapeDtypeStruct((1, rows), f32)
    lanes = 2 * HALF
    logprob, entropy = pl.pallas_call(
        kernel,
        out_shape=(out, out),
        in_specs=[hbm] * 7,
        out_specs=(vmem, vmem),
        scratch_shapes=[
            pltpu.SMEM(lengths.shape, jnp.int32),
            pltpu.SMEM(lengths.shape, jnp.int32),
            pltpu.SMEM(lengths.shape, jnp.int32),
            pltpu.VMEM((rows, features), bf16),
            pltpu.VMEM((1, features), f32),
            pltpu.VMEM((1, rows), jnp.int32),
            pltpu.VMEM((8 * width, features), bf16),
            pltpu.VMEM((NZ * lanes, features), bf16),
            pltpu.VMEM((NZ * lanes, features), bf16),
            pltpu.VMEM((NZ, 8, lanes), jnp.int32),
            pltpu.VMEM((4, 8, 2 * lanes), jnp.int32),
            pltpu.VMEM((NY, 8, features), bf16),
            pltpu.VMEM((NZ, NY, features), bf16),
            pltpu.VMEM((8, features), f32),
            pltpu.VMEM((4, 4, 8, 2 * lanes), f32),
            pltpu.VMEM((NZ, 8, lanes), f32),
            pltpu.VMEM((NZ, 8, lanes), f32),
            pltpu.VMEM((8, lanes), f32),
            pltpu.VMEM((NX * NC, 8, lanes), f32),
            pltpu.SemaphoreType.DMA((len(NUMBER),)),
            pltpu.SemaphoreType.DMA((len(NUMBER),)),
            pltpu.SemaphoreType.DMA((8,)),
            pltpu.SemaphoreType.REGULAR((RELAYS,)),
        ],
        compiler_params=pltpu.CompilerParams(
            collective_id=0, has_side_effects=True, vmem_limit_bytes=64 * 2**20
        ),
    )(
        lengths, prior_device, prior_row, hidden, norm_gain.reshape(1, features), head_weight.T,
        targets.reshape(1, rows),
    )
    return logprob.reshape(rows), entropy.reshape(rows)


def solution(mesh):
    in_specs = (P("tok", None), P(), P(None, ("tok", "voc")), P("tok"), P(), P(), P())
    out_specs = (P("tok"), P("tok"))
    return jax.shard_map(body, mesh=mesh, in_specs=in_specs, out_specs=out_specs, check_vma=False)
```

time: 56.6 us -> 50.8 us (0.90)
  Pallas kernels: 51.7 us -> 46.8 us
  local copies, waits for them, and re-layouts: 4.06 us -> 3.12 us
    pallas_call x1, Pallas kernels: 51.7 us -> 46.8 us  [body(): pl.pallas_call(kernel, out_shape=(out, out), in_specs=[hbm] * 7, out_spec...]
    unnamed x14 -> x6, local copies, waits for them, and re-layouts: 3.34 us -> 1.83 us
    reshape x1, local copies, waits for them, and re-layouts: 0.73 us -> 1.29 us  [body(): norm_gain.reshape(1, features)]
where the time goes in v2:
time: 50.8 us; the launch traced here: 50.6 us
  Pallas kernels  46.8 us (92%)
  local copies, waits for them, and re-layouts  3.12 us (6%)
  between operations  0.65 us (1%)
    pallas_call x1, Pallas kernels, body(): pl.pallas_call(kernel, out_shape=(out, out), in_specs=[hbm] * 7, out_spec...  46.8 us
    unnamed x6, local copies, waits for them, and re-layouts  1.83 us
    reshape x1, local copies, waits for them, and re-layouts, body(): norm_gain.reshape(1, features)  1.29 us

profile of v2, /device:TPU:1, one launch (start us, length us, event | category | flops | bytes accessed | tf_op | source)
XLA Modules:
  0.0 50.6 jit_solution(17872515508416711188)
XLA Ops:
  0.6 1.3 %reshape.16.gain_hbm = f32[1,1536]{1,0:T(1,128)} reshape(f32[1536]{0:T(1024)} %param.8) | data formatting | bytes 12288 | tf_op jit(solution)/shard_map/reshape | solution.py:530
  1.9 46.8 %shard_map.86 = (f32[1,256]{1,0:T(1,128)}, f32[1,256]{1,0:T(1,128)}) custom-call(s32[32]{0:T(128)} %lengths_hbm.1, s32[32]{0:T(128)} %device_hbm.1, s32[32]{0:T(128)} %row_hbm.1, bf16[256,1536]{1,0:T(8,128)(2,1)} %hidden_hbm.1, f32[1,1536]{1,0:T(1,128)} %reshape.16.gain_hbm, bf16[192,1536]{1,0:T(8,128)(2,1)} %bitcast.4, s32[1,256]{1,0:T(1,128)} %bitcast.5), custom_call_target="tpu_custom_call" | custom-call | tf_op jit(solution)/shard_map/pallas_call | solution.py:496
  48.8 0.0 copy-start.1
  48.8 0.6 %copy-done.1 = f32[1,256]{1,0:T(1,128)S(1)} copy-done((f32[1,256]{1,0:T(1,128)S(1)}, f32[1,256]{1,0:T(1,128)}, u32[]{:S(2)}) %copy-start.1) | copy-done | bytes 1048
  49.4 0.0 copy-start
  49.4 0.6 %copy.11 = f32[256]{0:T(256)} copy(f32[256]{0:T(256)S(1)} %bitcast.7) | data formatting | bytes 2048
  50.0 0.1 copy-done
  50.0 0.6 %copy.12 = f32[256]{0:T(256)} copy(f32[256]{0:T(256)S(1)} %bitcast.6) | data formatting | bytes 2048
Async XLA Ops:
  48.8 0.6 %copy-start.1 = (f32[1,256]{1,0:T(1,128)S(1)}, f32[1,256]{1,0:T(1,128)}, u32[]{:S(2)}) copy-start(f32[1,256]{1,0:T(1,128)} %get-tuple-element.4) | copy-start | bytes 3076
  49.4 0.6 %copy-start = (f32[1,256]{1,0:T(1,128)S(1)}, f32[1,256]{1,0:T(1,128)}, u32[]{:S(2)}) copy-start(f32[1,256]{1,0:T(1,128)} %get-tuple-element.5) | copy-start | bytes 3076

commit v3 on v2

--- a/solution.py
+++ b/solution.py
@@ -67,7 +67,7 @@
     fetches = [
         pltpu.make_async_copy(weight, wbuf.at[pl.ds(0, width)], local.at[0]),
         pltpu.make_async_copy(hidden_hbm.at[own_rows], hidden.at[own_rows], local.at[1]),
-        pltpu.make_async_copy(gain_hbm, gain, local.at[2]),
+        pltpu.make_async_copy(gain_hbm, gain.at[0], local.at[2]),
         pltpu.make_async_copy(hidden_hbm.at[other_rows], hidden.at[other_rows], local.at[3]),
         pltpu.make_async_copy(device_hbm, prior_device, local.at[4]),
         pltpu.make_async_copy(row_hbm, prior_row, local.at[5]),
@@ -207,33 +207,6 @@
     shifted = pltpu.roll(jnp.broadcast_to(targets[...], shape), shape[1] - 1, 1)
     straight = jnp.where(c == 0, shifted[:, :block], shifted[:, block:])
     tgt[0] = turned(straight)
-    pl.semaphore_wait(relay.at[0], 2)
-    tell(1, "dz")
-    norm_half(1 - kind)
-    prior[...] = jnp.zeros_like(prior)
-    for g in range(4):
-        stats[g, 0] = jnp.full(stats.shape[2:], LOWEST, jnp.float32)
-        for k in range(1, 4):
-            stats[g, k] = jnp.zeros(stats.shape[2:], jnp.float32)
-    pl.semaphore_wait(relay.at[1], 2)
-    tell(2, "dz")
-    pl.semaphore_wait(relay.at[3], 2)
-    for d in range(1, NY):
-        row_y_message(d).wait_recv()
-    gathered = row_y[0].astype(jnp.float32)
-    for d in range(1, NY):
-        gathered = gathered + row_y[d].astype(jnp.float32)
-    pl.semaphore_wait(relay.at[2], 2)
-
-    @pl.when(c == 1)
-    def _():
-        row_z[z] = gathered[:NY].astype(jnp.bfloat16)
-        for s in range(1, NZ):
-            row_z_message(s).start()
-
-    for s in range(1, NZ):
-        start(target_message, s)
-
     def pass_on(k, late):
         for side in "rl":
             p = late if side == "r" else 1 - late
@@ -241,6 +214,33 @@
             if k < 2 or (k == 2 and late == 0):
                 start(along_z, side, k + 1, p)
             start(along_x, target_slot[side][k], p)
+
+    pl.semaphore_wait(relay.at[0], 2)
+    tell(1, "dz")
+    norm_half(1 - kind)
+    pl.semaphore_wait(relay.at[1], 2)
+    tell(2, "dz")
+    for d in range(1, NY):
+        row_y_message(d).wait_recv()
+    gathered = row_y[0].astype(jnp.float32)
+    for d in range(1, NY):
+        gathered = gathered + row_y[d].astype(jnp.float32)
+    pl.semaphore_wait(relay.at[3], 2)
+    pl.semaphore_wait(relay.at[2], 2)
+
+    @pl.when(c == 1)
+    def _():
+        row_z[z] = gathered[:NY].astype(jnp.bfloat16)
+        for s in range(1, NZ):
+            row_z_message(s).start()
+
+    for s in range(1, NZ):
+        start(target_message, s)
+    prior[...] = jnp.zeros_like(prior)
+    for g in range(4):
+        stats[g, 0] = jnp.full(stats.shape[2:], LOWEST, jnp.float32)
+        for k in range(1, 4):
+            stats[g, k] = jnp.zeros(stats.shape[2:], jnp.float32)
 
     def whole(slot):
         for p in range(2):
@@ -524,11 +524,15 @@
             pltpu.SemaphoreType.REGULAR((RELAYS,)),
         ],
         compiler_params=pltpu.CompilerParams(
-            collective_id=0, has_side_effects=True, vmem_limit_bytes=64 * 2**20
+            collective_id=0, has_side_effects=True, vmem_limit_bytes=48 * 2**20
         ),
     )(
-        lengths, prior_device, prior_row, hidden, norm_gain.reshape(1, features), head_weight.T,
-        targets.reshape(1, rows),
+        *[
+            pltpu.with_memory_space_constraint(operand, pltpu.HBM)
+            for operand in (
+                lengths, prior_device, prior_row, hidden, norm_gain, head_weight.T, targets.reshape(1, rows)
+            )
+        ]
     )
     return logprob.reshape(rows), entropy.reshape(rows)
 

time: 50.8 us -> 48.3 us (0.951)
  local copies, waits for them, and re-layouts: 3.12 us -> 1.13 us
    reshape x1 -> x0, local copies, waits for them, and re-layouts: 1.29 us -> none  [body(): norm_gain.reshape(1, features)]
    unnamed x6 -> x2, local copies, waits for them, and re-layouts: 1.83 us -> 1.13 us
where the time goes in v3:
time: 48.3 us; the launch traced here: 48.2 us
  Pallas kernels  46.4 us (96%)
  local copies, waits for them, and re-layouts  1.13 us (2%)
  between operations  0.64 us (1%)
    pallas_call x1, Pallas kernels, body(): pl.pallas_call(kernel, out_shape=(out, out), in_specs=[hbm] * 7, out_spec...  46.4 us
    unnamed x2, local copies, waits for them, and re-layouts  1.13 us

profile of v3, /device:TPU:1, one launch (start us, length us, event | category | flops | bytes accessed | tf_op | source)
XLA Modules:
  0.0 48.2 jit_solution(1589983076213683262)
XLA Ops:
  0.6 46.4 %shard_map.86 = (f32[1,256]{1,0:T(1,128)S(1)}, f32[1,256]{1,0:T(1,128)S(1)}) custom-call(s32[32]{0:T(128)} %lengths_hbm.1, s32[32]{0:T(128)} %device_hbm.1, s32[32]{0:T(128)} %row_hbm.1, bf16[256,1536]{1,0:T(8,128)(2,1)} %hidden_hbm.1, f32[1536]{0:T(1024)} %gain_hbm.1, bf16[192,1536]{1,0:T(8,128)(2,1)} %bitcast.6, s32[1,256]{1,0:T(1,128)} %bitcast.7), custom_call_target="tpu_custom_call" | custom-call | tf_op jit(solution)/shard_map/pallas_call | solution.py:496
  47.1 0.6 %copy.11 = f32[256]{0:T(256)} copy(f32[256]{0:T(256)S(1)} %bitcast.5) | data formatting | bytes 2048
  47.6 0.6 %copy.12 = f32[256]{0:T(256)} copy(f32[256]{0:T(256)S(1)} %bitcast.4) | data formatting | bytes 2048

commit v4 on v3

--- a/solution.py
+++ b/solution.py
@@ -184,6 +184,13 @@
     fetches[0].wait()
 
     pl.semaphore_wait(barrier, len(PEERS))
+    def tell(level, axis):
+        for d in (1, -1):
+            pl.semaphore_signal(relay.at[level], inc=1, device_id=peer(**{axis: d}), device_id_type=MESH)
+
+    tell(0, "dz")
+    tell(3, "dx")
+
     for d in range(1, NY):
         start(row_y_message, d)
     for p in range(2):
@@ -193,13 +200,6 @@
         for side in "rl":
             start(weights, (side, part))
     start(weights, "own_s")
-
-    def tell(level, axis):
-        for d in (1, -1):
-            pl.semaphore_signal(relay.at[level], inc=1, device_id=peer(**{axis: d}), device_id_type=MESH)
-
-    tell(0, "dz")
-    tell(3, "dx")
 
     def turned(value):
         return jnp.where(kind == 0, value, pltpu.roll(value, HALF, 1))
@@ -217,9 +217,9 @@
 
     pl.semaphore_wait(relay.at[0], 2)
     tell(1, "dz")
-    norm_half(1 - kind)
     pl.semaphore_wait(relay.at[1], 2)
     tell(2, "dz")
+    norm_half(1 - kind)
     for d in range(1, NY):
         row_y_message(d).wait_recv()
     gathered = row_y[0].astype(jnp.float32)

time: 48.3 us -> 48.3 us (level)
  no operation moved by 1% of the time
where the time goes in v4:
time: 48.3 us; the launch traced here: 48.2 us
  Pallas kernels  46.4 us (96%)
  local copies, waits for them, and re-layouts  1.13 us (2%)
  between operations  0.64 us (1%)
    pallas_call x1, Pallas kernels, body(): pl.pallas_call(kernel, out_shape=(out, out), in_specs=[hbm] * 7, out_spec...  46.4 us
    unnamed x2, local copies, waits for them, and re-layouts  1.13 us

profile of v4, /device:TPU:1, one launch (start us, length us, event | category | flops | bytes accessed | tf_op | source)
XLA Modules:
  0.0 48.2 jit_solution(16488785210376239439)
XLA Ops:
  0.6 46.4 %shard_map.86 = (f32[1,256]{1,0:T(1,128)S(1)}, f32[1,256]{1,0:T(1,128)S(1)}) custom-call(s32[32]{0:T(128)} %lengths_hbm.1, s32[32]{0:T(128)} %device_hbm.1, s32[32]{0:T(128)} %row_hbm.1, bf16[256,1536]{1,0:T(8,128)(2,1)} %hidden_hbm.1, f32[1536]{0:T(1024)} %gain_hbm.1, bf16[192,1536]{1,0:T(8,128)(2,1)} %bitcast.6, s32[1,256]{1,0:T(1,128)} %bitcast.7), custom_call_target="tpu_custom_call" | custom-call | tf_op jit(solution)/shard_map/pallas_call | solution.py:496
  47.1 0.6 %copy.11 = f32[256]{0:T(256)} copy(f32[256]{0:T(256)S(1)} %bitcast.5) | data formatting | bytes 2048
  47.6 0.6 %copy.12 = f32[256]{0:T(256)} copy(f32[256]{0:T(256)S(1)} %bitcast.4) | data formatting | bytes 2048
